TPU v7x, 256 devices: a whole 4x4x8 slice. The times are simulated.
256 devices in a mesh: pair: 16 (over z_hi, y, core), aux: 16 (over x, z_lo).
Axes of the slice: x: 4, y: 4, z: 8 (z_hi: 2, z_lo: 4; z = z_hi * 4 + z_lo), core: 2. Of those that a mesh axis runs over, the one named last changes fastest.
Arguments:
- three_index: float32 [32, 768, 8192], P('pair', None, 'aux'), may hold values from -0.6 to 0.6
- occupied_energy: float32 [32], P('pair'), may hold values from -2 to -0.5
- virtual_energy: float32 [768], replicated, may hold values from 0.2 to 3
- plan: int32 [2, 32], P(None, 'pair'), may hold values from 0 to 1, as said below
Outputs:
- gradient_blocks: float32 [32, 768, 8192], P('pair', None, 'aux')
- virtual_density: float32 [768, 768], P('aux', 'pair')
Inputs may be any that keep to these rules, and one draw needn't show every extreme that they name: For block p and round r with q = p XOR 2**r: the row plan[r, p * 2 : (p + 1) * 2] is a permutation of the slots, and plan[r, q * 2 + plan[r, p * 2 + k]] = k, so every orbital is paired with exactly one orbital of block q in each round.
All inputs are finite; a program needn't handle non-finite values.
Results may differ from a plain program's by a relative error of at most 0.0001.
Values sent between devices are 32-bit elements; how exact they have to be, the bound alone decides.
A program may use at most 128 MiB of HBM per device.

v0:
```python
import jax
import jax.numpy as jnp
from jax import lax
from jax.sharding import PartitionSpec as P


def swapped(block, axis, bit):
    count = lax.axis_size(axis)
    route = []
    for low in range(count):
        high = low | 1 << bit
        if high != low and high < count:
            route += [(low, high), (high, low)]
    return lax.ppermute(block, axis, route)


def body(three_index, occupied_energy, virtual_energy, plan):
    highest = lax.Precision.HIGHEST
    per_block = three_index.shape[0]
    half_count = per_block // 2
    width = three_index.shape[1]
    row_count = width // lax.axis_size("aux")
    row_start = lax.axis_index("aux") * row_count
    position = lax.axis_index("pair")
    slots = jnp.arange(per_block, dtype=jnp.int32)
    lower_slots = slots[:half_count]
    upper_slots = slots[half_count:]
    gradient = jnp.zeros(three_index.shape, jnp.float32)
    density = jnp.zeros((row_count, width), jnp.float32)
    for turn_index in range(plan.shape[0]):
        table = plan[turn_index]
        upper_side = position // 2**turn_index % 2 == 1
        inverse = jnp.sum(jnp.where(table[None, :] == slots[:, None], slots[None, :], 0), axis=1)
        own_slots = jnp.where(upper_side, inverse[half_count:], lower_slots)
        peer_slots = jnp.where(upper_side, upper_slots, table[:half_count])
        send_slots = jnp.where(upper_side, inverse[:half_count], upper_slots)
        own_blocks = jnp.take(three_index, own_slots, axis=0)
        own_energy = jnp.take(occupied_energy, own_slots)
        peer_all, energy_all = swapped((three_index, occupied_energy), "pair", turn_index)
        peer_blocks = jnp.take(peer_all, peer_slots, axis=0)
        peer_energy = jnp.take(energy_all, peer_slots)
        pair_energy = own_energy + peer_energy
        partial_value = jnp.einsum(
            "hap,hbp->ahb",
            own_blocks,
            peer_blocks,
            precision=highest,
            preferred_element_type=jnp.float32,
        )
        summed = lax.psum(partial_value, "aux")
        gap_full = (
            pair_energy[None, :, None]
            - virtual_energy[:, None, None]
            - virtual_energy[None, None, :]
        )
        amplitude = summed / gap_full
        tilde = 2.0 * amplitude - jnp.transpose(amplitude, (2, 1, 0))
        amp_rows = lax.dynamic_slice_in_dim(amplitude, row_start, row_count, 0)
        amp_columns = lax.dynamic_slice_in_dim(amplitude, row_start, row_count, 2)
        density = density + jnp.einsum(
            "ahc,bhc->ab", amp_rows, tilde, precision=highest, preferred_element_type=jnp.float32
        )
        density = density + jnp.einsum(
            "cha,chb->ab", amp_columns, tilde, precision=highest, preferred_element_type=jnp.float32
        )
        own_term = jnp.einsum(
            "ahb,hbp->hap",
            tilde,
            peer_blocks,
            precision=highest,
            preferred_element_type=jnp.float32,
        )
        peer_term = jnp.einsum(
            "ahb,hap->hbp", tilde, own_blocks, precision=highest, preferred_element_type=jnp.float32
        )
        returned = swapped(peer_term, "pair", turn_index)
        gradient = gradient.at[own_slots].add(own_term)
        gradient = gradient.at[send_slots].add(returned)
    density = lax.psum_scatter(density, "pair", scatter_dimension=1, tiled=True)
    return (gradient, density)


def solution(mesh):
    in_specs = (P("pair", None, "aux"), P("pair"), P(), P(None, "pair"))
    out_specs = (P("pair", None, "aux"), P("aux", "pair"))
    return jax.shard_map(body, mesh=mesh, in_specs=in_specs, out_specs=out_specs, check_vma=False)
```

profile of v0, /device:TPU:2, one launch (start us, length us, event | category | flops | bytes accessed | tf_op | source)
XLA Modules:
  0.0 451.5 jit_solution(10524392798623498606)
XLA Ops:
  7.3 1.7 collective-permute-start.3
  9.0 0.8 slice_bitcast_fusion
  11.1 0.6 slice.125
  11.8 1.3 fusion.94
  17.0 7.9 %convolution_bitcast_fusion.1 = f32[768,1,768]{0,2,1:T(8,128)} fusion(f32[2,768,512]{2,1,0:T(8,128)S(1)} %collective-permute-done, s32[]{:T(128)} %bitcast.4, f32[2,768,512]{2,1,0:T(8,128)} %param.14, s32[]{:T(128)} %bitcast.7, pred[]{:T(512)} %bitcast.6, pred[]{:T(512)} %bitcast.3), kind=kOutput, calls=%fused_computation.24 | convolution fusion | flops 3624665088 | bytes 5507072 | tf_op jit(solution)/shard_map/hap,hbp->ahb/dot_general | solution.py:43
  25.0 53.2 %collective-permute-done.3 = f32[2,768,512]{2,1,0:T(8,128)} collective-permute-done((f32[2,768,512]{2,1,0:T(8,128)}, f32[2,768,512]{2,1,0:T(8,128)}, u32[]{:S(2)}, u32[]{:S(2)}) %collective-permute-start.3) | collective-permute-done | bytes 3145760 | tf_op jit(solution)/shard_map/ppermute | solution.py:14
  78.1 6.9 %convolution_bitcast_fusion = f32[768,1,768]{0,2,1:T(8,128)} fusion(f32[2,768,512]{2,1,0:T(8,128)} %collective-permute-done.3, s32[]{:T(128)} %bitcast.24, f32[2,768,512]{2,1,0:T(8,128)S(1)} %copy-done.3, s32[]{:T(128)} %bitcast.21, pred[]{:T(512)} %bitcast.26, pred[]{:T(512)} %bitcast.23), kind=kOutput, calls=%fused_computation.23 | convolution fusion | flops 3624665088 | bytes 5507072 | tf_op jit(solution)/shard_map/hap,hbp->ahb/dot_general | solution.py:43
  85.7 1.6 collective-permute-start.4
  91.9 0.8 and_reduce_fusion
  95.2 213.8 %all-reduce.3.cloned.1.call-done = (f32[768,1,768]{0,2,1:T(8,128)}, f32[768,1,768]{0,2,1:T(8,128)}) async-done(((f32[768,1,768]{0,2,1:T(8,128)}, f32[768,1,768]{0,2,1:T(8,128)}), (f32[768,1,768]{0,2,1:T(8,128)}, f32[768,1,768]{0,2,1:T(8,128)})) %all-reduce.3.cloned.1.call-update) | async-done | bytes 4718608 | tf_op jit(solution)/shard_map/psum | solution.py:50
  309.0 4.5 subtract_divide_fusion
  313.5 1.5 copy-done.2
  315.0 2.0 copy.10
  317.0 2.8 bitcast_subtract_fusion.1
  320.3 5.0 %fusion.27 = f32[1,768,512]{2,1,0:T(8,128)} fusion(f32[768,1,768]{2,0,1:T(8,128)S(1)} %bitcast_subtract_fusion.1, f32[2,768,512]{2,1,0:T(8,128)S(1)} %copy-done.4, s32[]{:T(128)} %bitcast.7, pred[]{:T(512)} %bitcast.6), kind=kOutput, calls=%fused_computation.41 | convolution fusion | flops 3624271872 | bytes 5505029 | tf_op jit(solution)/shard_map/ahb,hap->hbp/dot_general | solution.py:73
  325.4 3.1 copy.11
  328.5 2.8 bitcast_subtract_fusion
  331.8 5.1 %fusion.32 = f32[1,768,512]{2,1,0:T(8,128)} fusion(f32[768,1,768]{2,0,1:T(8,128)S(1)} %bitcast_subtract_fusion, f32[2,768,512]{2,1,0:T(8,128)S(1)} %copy-done.5, s32[]{:T(128)} %bitcast.21, pred[]{:T(512)} %bitcast.26), kind=kOutput, calls=%fused_computation.42 | convolution fusion | flops 3624271872 | bytes 5505029 | tf_op jit(solution)/shard_map/ahb,hap->hbp/dot_general | solution.py:73
  336.9 1.6 collective-permute-start.5
  338.5 3.4 fusion.2
  341.9 2.4 fusion.8
  344.3 3.3 fusion.48
  347.7 2.4 fusion.51
  350.1 1.0 copy.12
  351.1 2.1 broadcast_in_dim.57
  353.2 1.0 copy-done.7
  354.2 5.6 %bitcast_dynamic-update-slice_fusion = f32[2,768,512]{2,1,0:T(8,128)} fusion(f32[2,768,512]{2,1,0:T(8,128)} %broadcast_in_dim.57, s32[]{:T(128)} %bitcast.7, f32[768,1,768]{2,0,1:T(8,128)S(1)} %bitcast_subtract_fusion.1, f32[2,768,512]{2,1,0:T(8,128)S(1)} %copy-done.7, s32[]{:T(128)} %bitcast.4, pred[]{:T(512)} %bitcast.3, pred[]{:T(512)} %get-tuple-element.120), kind=kOutput, calls=%fused_computation.32 | convolution fusion | flops 3624665088 | bytes 5507072 | tf_op jit(solution)/shard_map/ahb,hbp->hap/dot_general | solution.py:66
  359.7 67.2 %reduce-scatter.4.cloned.1.call-done = f32[48,48]{1,0:T(8,128)} async-done(((f32[768,48]{1,0:T(8,128)}), f32[48,48]{1,0:T(8,128)}) %reduce-scatter.4.cloned.1.call-update) | async-done | bytes 9232
  427.0 1.4 copy.13
  428.4 4.2 fusion.16
  432.6 7.8 %fusion.17 = f32[2,768,512]{2,1,0:T(8,128)} fusion(f32[2,768,512]{2,1,0:T(8,128)} %fusion.16, s32[]{:T(128)} %bitcast.21, f32[2,768,512]{2,1,0:T(8,128)} %collective-permute-done.3, s32[]{:T(128)} %bitcast.24, f32[768,1,768]{2,0,1:T(8,128)S(1)} %copy-done.1, pred[]{:T(512)} %bitcast.23, pred[]{:T(512)} %get-tuple-element.107), kind=kOutput, calls=%fused_computation.26 | convolution fusion | flops 3625058304 | bytes 7079936 | tf_op jit(solution)/shard_map/ahb,hbp->hap/dot_general | solution.py:66
  440.4 4.0 fusion.18
  (41 shorter events, 5.3 us)
Async XLA Ops:
  7.2 301.8 %all-reduce.3.cloned.1.call-start = ((), (), s32[]{:S(2)}) async-start(), calls=%async_computation.2 | async-start | bytes 9437184 | tf_op jit(solution)/shard_map/psum | solution.py:50
  7.2 9.8 %collective-permute-start = (f32[2,768,512]{2,1,0:T(8,128)}, f32[2,768,512]{2,1,0:T(8,128)S(1)}, u32[]{:S(2)}, u32[]{:S(2)}) collective-permute-start(f32[2,768,512]{2,1,0:T(8,128)} %param.14), channel_id=1, source_target_pairs={{0,16},{16,0},{32,48},{48,32},{64,80},{80,64},{96,112},{112,96},{1... | collective-permute-start | bytes 9437192 | tf_op jit(solution)/shard_map/ppermute | solution.py:14
  7.3 70.8 %collective-permute-start.3 = (f32[2,768,512]{2,1,0:T(8,128)}, f32[2,768,512]{2,1,0:T(8,128)}, u32[]{:S(2)}, u32[]{:S(2)}) collective-permute-start(f32[2,768,512]{2,1,0:T(8,128)} %param.14), channel_id=1, source_target_pairs={{0,32},{32,0},{16,48},{48,16},{64,96},{96,64},{80,112},{112,80},{1... | collective-permute-start | bytes 9437192 | tf_op jit(solution)/shard_map/ppermute | solution.py:14
  17.0 8.0 %copy-start.6 = (f32[2,768,512]{2,1,0:T(8,128)}, f32[2,768,512]{2,1,0:T(8,128)S(1)}, u32[]{:S(2)}) copy-start(f32[2,768,512]{2,1,0:T(8,128)S(1)} %collective-permute-done) | copy-start | bytes 9437188
  17.0 61.1 %copy-start.3 = (f32[2,768,512]{2,1,0:T(8,128)S(1)}, f32[2,768,512]{2,1,0:T(8,128)}, u32[]{:S(2)}) copy-start(f32[2,768,512]{2,1,0:T(8,128)} %param.14) | copy-start | bytes 9437188
  85.0 0.7 copy-start.9
  85.0 6.9 %copy-start.10 = (s32[3]{0:T(128)S(1)}, s32[3]{0:T(128)}, u32[]{:S(2)}) copy-start(s32[3]{0:T(128)} %constant.173.clone.1) | copy-start | bytes 40
  85.0 10.2 %copy-start.8 = (f32[768]{0:T(1024)S(1)}, f32[768]{0:T(1024)}, u32[]{:S(2)}) copy-start(f32[768]{0:T(1024)} %param.16) | copy-start | bytes 9220
  85.0 342.0 %reduce-scatter.4.cloned.1.call-start = ((), (), s32[]{:S(2)}) async-start(), calls=%async_computation.1 | async-start | bytes 417792
  85.7 7.0 %collective-permute-start.4 = (f32[2]{0:T(128)S(1)}, f32[2]{0:T(128)S(1)}, u32[]{:S(2)}, u32[]{:S(2)}) collective-permute-start(f32[2]{0:T(128)S(1)} %copy-done.9), channel_id=1, source_target_pairs={{0,32},{32,0},{16,48},{48,16},{64,96},{96,64},{80,112},{112,80},{1... | collective-permute-start | bytes 32 | tf_op jit(solution)/shard_map/ppermute | solution.py:14
  87.2 6.7 %collective-permute-start.1 = (f32[2]{0:T(128)S(1)}, f32[2]{0:T(128)S(1)}, u32[]{:S(2)}, u32[]{:S(2)}) collective-permute-start(f32[2]{0:T(128)S(1)} %copy-done.9), channel_id=1, source_target_pairs={{0,16},{16,0},{32,48},{48,32},{64,80},{80,64},{96,112},{112,96},{1... | collective-permute-start | bytes 32 | tf_op jit(solution)/shard_map/ppermute | solution.py:14
  313.5 1.5 copy-start.2
  317.0 3.3 copy-start.4
  325.4 103.0 %collective-permute-start.2 = (f32[1,768,512]{2,1,0:T(8,128)}, f32[1,768,512]{2,1,0:T(8,128)}, u32[]{:S(2)}, u32[]{:S(2)}) collective-permute-start(f32[1,768,512]{2,1,0:T(8,128)} %fusion.27), channel_id=1, source_target_pairs={{0,16},{16,0},{32,48},{48,32},{64,80},{80,64},{96,112},{112,96},{1... | collective-permute-start | bytes 4718600 | tf_op jit(solution)/shard_map/ppermute | solution.py:14
  328.5 3.3 copy-start.5
  331.8 15.9 %copy-start = (f32[768,1,768]{2,0,1:T(8,128)}, f32[768,1,768]{2,0,1:T(8,128)S(1)}, u32[]{:S(2)}) copy-start(f32[768,1,768]{2,0,1:T(8,128)S(1)} %bitcast_subtract_fusion) | copy-start | bytes 7077892
  336.9 103.5 %collective-permute-start.5 = (f32[1,768,512]{2,1,0:T(8,128)}, f32[1,768,512]{2,1,0:T(8,128)}, u32[]{:S(2)}, u32[]{:S(2)}) collective-permute-start(f32[1,768,512]{2,1,0:T(8,128)} %fusion.32), channel_id=1, source_target_pairs={{0,32},{32,0},{16,48},{48,16},{64,96},{96,64},{80,112},{112,80},{1... | collective-permute-start | bytes 4718600 | tf_op jit(solution)/shard_map/ppermute | solution.py:14
  351.1 3.0 copy-start.7
  428.4 4.2 copy-start.1
Sparse Core Ops, SparseCore 0:
  85.1 223.8 all-reduce.2
  351.2 75.6 reduce-scatter.3
where the time goes:
time: 459 us; the launch traced here: 451 us
  waiting for transfers between devices  334 us (73%)
  matrix products  49.8 us (11%)
  between operations  23.3 us (5%)
  local copies, waits for them, and re-layouts  19.3 us (4%)
  other arithmetic  19.3 us (4%)
  starting transfers between devices  5.5 us (1%)
    psum x1, waiting for transfers between devices, body(): summed = lax.psum(partial_value, 'aux')  214 us
    unnamed x3, waiting for transfers between devices  67.3 us
    ppermute x6, waiting for transfers between devices, swapped(): return lax.ppermute(block, axis, route)  53.2 us
    dot_general x2, matrix products, body(): jnp.einsum('hap,hbp->ahb', own_blocks, peer_blocks, precision=highest, pr...  14.8 us
    dot_general x2, matrix products, body(): jnp.einsum('ahb,hbp->hap', tilde, peer_blocks, precision=highest, preferr...  13.4 us
    dot_general x2, matrix products, body(): jnp.einsum('ahb,hap->hbp', tilde, own_blocks, precision=highest, preferre...  10.1 us
  transfers between devices with their start and end apart: 8, of which 3 were waited for; matrix products, arithmetic and copies ran while one was open for 13% of the time, Pallas kernels for 0%

commit v1 on v0

--- a/solution.py
+++ b/solution.py
@@ -47,7 +47,7 @@
             precision=highest,
             preferred_element_type=jnp.float32,
         )
-        summed = lax.psum(partial_value, "aux")
+        summed = jnp.sum(lax.all_gather(partial_value, "aux"), axis=0)
         gap_full = (
             pair_energy[None, :, None]
             - virtual_energy[:, None, None]

time: 459 us -> 1830 us (3.99)
  waiting for transfers between devices: 334 us -> 1630 us
  local copies, waits for them, and re-layouts: 19.3 us -> 63.8 us
  other arithmetic: 19.3 us -> 51.5 us
    all_gather x0 -> x2, waiting for transfers between devices: none -> 1490 us  [body(): summed = jnp.sum(lax.all_gather(partial_value, 'aux'), axis=0)]
    psum x1 -> x0, waiting for transfers between devices: 214 us -> none  [body(): summed = lax.psum(partial_value, 'aux')]
    unnamed x24 -> x22, local copies, waits for them, and re-layouts: 6.39 us -> 50.9 us
    reduce_sum x0 -> x2, other arithmetic: none -> 32.4 us  [body(): summed = jnp.sum(lax.all_gather(partial_value, 'aux'), axis=0)]
    unnamed x3 -> x4, waiting for transfers between devices: 67.3 us -> 70.9 us
  transfers between devices with their start and end apart: 8 -> 9, of which waited for: 3 -> 5; matrix products, arithmetic and copies ran while one was open for 13% -> 5% of each run, Pallas kernels for 0% -> 0%
where the time goes in v1:
time: 1830 us; the launch traced here: 1820 us
  waiting for transfers between devices  1630 us (89%)
  local copies, waits for them, and re-layouts  63.8 us (3%)
  other arithmetic  51.5 us (3%)
  matrix products  50.7 us (3%)
  between operations  23.3 us (1%)
    all_gather x2, waiting for transfers between devices, body(): summed = jnp.sum(lax.all_gather(partial_value, 'aux'), axis=0)  1490 us
    unnamed x4, waiting for transfers between devices  70.9 us
    ppermute x6, waiting for transfers between devices, swapped(): return lax.ppermute(block, axis, route)  66.4 us
    unnamed x22, local copies, waits for them, and re-layouts  50.9 us
  transfers between devices with their start and end apart: 9, of which 5 were waited for; matrix products, arithmetic and copies ran while one was open for 5% of the time, Pallas kernels for 0%

profile of v1, /device:TPU:2, one launch (start us, length us, event | category | flops | bytes accessed | tf_op | source)
XLA Modules:
  0.0 1823.4 jit_solution(5636491314039703679)
XLA Ops:
  7.2 1.7 collective-permute-start.3
  14.3 63.0 %collective-permute-done.3 = f32[2,768,512]{2,1,0:T(8,128)S(1)} collective-permute-done((f32[2,768,512]{2,1,0:T(8,128)}, f32[2,768,512]{2,1,0:T(8,128)S(1)}, u32[]{:S(2)}, u32[]{:S(2)}) %collective-permute-start.3) | collective-permute-done | bytes 3145760 | tf_op jit(solution)/shard_map/ppermute | solution.py:14
  77.3 1.6 copy-done.5
  79.0 7.4 convolution_bitcast_fusion
  89.0 3.3 collective-permute-done
  92.4 6.8 convolution_bitcast_fusion.1
  99.8 1.6 collective-permute-start.4
  109.8 752.1 %all-gather.7.cloned.1.call-done = f32[12288,1,768]{0,2,1:T(8,128)} async-done(((f32[768,1,768]{0,2,1:T(8,128)}), f32[12288,1,768]{0,2,1:T(8,128)}) %all-gather.7.cloned.1.call-update) | async-done | bytes 37748752 | tf_op jit(solution)/shard_map/all_gather | solution.py:50
  861.9 22.4 %copy.15 = f32[96,8,16,768]{3,2,1,0:T(8,128)S(1)} copy(f32[96,8,16,768]{3,1,2,0:T(8,128)} %bitcast.135) | data formatting | bytes 75497472
  884.3 16.2 bitcast_reduce_fusion
  900.5 739.1 %all-gather.5.cloned.1.call-done = f32[12288,1,768]{0,2,1:T(8,128)} async-done(((f32[768,1,768]{0,2,1:T(8,128)}), f32[12288,1,768]{0,2,1:T(8,128)}) %all-gather.5.cloned.1.call-update) | async-done | bytes 37748752 | tf_op jit(solution)/shard_map/all_gather | solution.py:50
  1639.5 22.0 %copy.14 = f32[96,8,16,768]{3,2,1,0:T(8,128)S(1)} copy(f32[96,8,16,768]{3,1,2,0:T(8,128)} %bitcast.136) | data formatting | bytes 75497472
  1661.6 16.2 bitcast_reduce_fusion.1
  1677.8 4.5 bitcast_divide_fusion
  1683.7 1.9 copy.10
  1685.6 2.7 bitcast_subtract_fusion.1
  1688.3 3.2 copy.11
  1691.5 2.8 bitcast_subtract_fusion
  1694.8 5.0 fusion.27
  1699.9 5.1 fusion.32
  1704.9 1.7 collective-permute-start.5
  1706.6 2.4 fusion.8
  1709.0 3.4 fusion.2
  1712.4 3.3 fusion.48
  1715.8 2.4 fusion.51
  1719.2 2.1 broadcast_in_dim.57
  1721.2 7.0 bitcast_dynamic-update-slice_fusion
  1728.2 70.9 %reduce-scatter.4.cloned.1.call-done = f32[48,48]{1,0:T(8,128)} async-done(((f32[768,48]{1,0:T(8,128)}), f32[48,48]{1,0:T(8,128)}) %reduce-scatter.4.cloned.1.call-update) | async-done | bytes 9232
  1799.1 1.4 copy.13
  1800.5 4.2 fusion.16
  1804.7 7.9 fusion.17
  1812.6 4.1 fusion.18
  (44 shorter events, 10.8 us)
Async XLA Ops:
  7.2 854.7 %all-gather.7.cloned.1.call-start = ((), (), s32[]{:S(2)}) async-start(), calls=%async_computation.2 | async-start | bytes 40108032 | tf_op jit(solution)/shard_map/all_gather | solution.py:50
  7.2 70.1 %collective-permute-start.3 = (f32[2,768,512]{2,1,0:T(8,128)}, f32[2,768,512]{2,1,0:T(8,128)S(1)}, u32[]{:S(2)}, u32[]{:S(2)}) collective-permute-start(f32[2,768,512]{2,1,0:T(8,128)} %param.14), channel_id=1, source_target_pairs={{0,32},{32,0},{16,48},{48,16},{64,96},{96,64},{80,112},{112,80},{1... | collective-permute-start | bytes 9437192 | tf_op jit(solution)/shard_map/ppermute | solution.py:14
  77.3 1.6 copy-start.5
  79.0 7.5 copy-start.3
  86.4 1553.1 %all-gather.5.cloned.1.call-start = ((), (), s32[]{:S(2)}) async-start(), calls=%async_computation.1 | async-start | bytes 40108032 | tf_op jit(solution)/shard_map/all_gather | solution.py:50
  86.5 5.9 collective-permute-start
  99.1 0.7 copy-start.7
  99.1 7.3 copy-start.8
  99.1 10.6 copy-start.6
  99.2 1699.9 %reduce-scatter.4.cloned.1.call-start = ((), (), s32[]{:S(2)}) async-start(), calls=%async_computation.3 | async-start | bytes 417792
  99.8 7.5 collective-permute-start.4
  101.4 7.1 collective-permute-start.1
  1682.3 1.4 copy-start.2
  1691.5 3.3 copy-start.4
  1694.8 21.0 %copy-start = (f32[768,1,768]{2,0,1:T(8,128)}, f32[768,1,768]{2,0,1:T(8,128)S(1)}, u32[]{:S(2)}) copy-start(f32[768,1,768]{2,0,1:T(8,128)S(1)} %bitcast_subtract_fusion) | copy-start | bytes 7077892
  1699.9 100.6 %collective-permute-start.2 = (f32[1,768,512]{2,1,0:T(8,128)}, f32[1,768,512]{2,1,0:T(8,128)}, u32[]{:S(2)}, u32[]{:S(2)}) collective-permute-start(f32[1,768,512]{2,1,0:T(8,128)} %fusion.27), channel_id=1, source_target_pairs={{0,16},{16,0},{32,48},{48,32},{64,80},{80,64},{96,112},{112,96},{1... | collective-permute-start | bytes 4718600 | tf_op jit(solution)/shard_map/ppermute | solution.py:14
  1704.9 107.6 %collective-permute-start.5 = (f32[1,768,512]{2,1,0:T(8,128)}, f32[1,768,512]{2,1,0:T(8,128)}, u32[]{:S(2)}, u32[]{:S(2)}) collective-permute-start(f32[1,768,512]{2,1,0:T(8,128)} %fusion.32), channel_id=1, source_target_pairs={{0,32},{32,0},{16,48},{48,16},{64,96},{96,64},{80,112},{112,80},{1... | collective-permute-start | bytes 4718600 | tf_op jit(solution)/shard_map/ppermute | solution.py:14
  1800.5 4.2 copy-start.1
Sparse Core Ops, SparseCore 0:
  86.5 775.2 all-gather.6
  863.7 775.8 all-gather.4
  1719.3 79.7 reduce-scatter.3
